TPU v7x, 32 devices: a whole 2x2x4 slice. The times are simulated.
32 devices in a mesh: grp: 4 (over z), seq: 8 (over y, x, core).
Axes of the slice: x: 2, y: 2, z: 4, core: 2. Of those that a mesh axis runs over, the one named last changes fastest.
Arguments:
- tokens: bfloat16 [4096, 2048], P(('grp', 'seq')), may hold values from -6 to 6
- norm_gains: float32 [2, 2048], replicated, may hold values from 0.5 to 1.5
- norm_biases: float32 [2, 2048], replicated, may hold values from -1 to 1
- mix_weight: bfloat16 [2048, 3, 2048], P(None, None, 'seq'), may hold values from -0.125 to 0.125
- mix_bias: bfloat16 [3, 2048], P(None, 'seq'), may hold values from -1.796875 to 1.796875
- out_weight: bfloat16 [2048, 2048], P('seq'), may hold values from -0.5 to 0.5
- gate_up_weight: bfloat16 [2048, 2, 5632], P(None, None, 'seq'), may hold values from -0.125 to 0.125
- down_weight: bfloat16 [5632, 2048], P('seq'), may hold values from -0.078125 to 0.078125
- row_lengths: int32 [8], replicated, may hold values from 128 to 1024, as said below
- row_group: int32 [8], replicated, may hold values from 0 to 3, as said below
- cotangent: bfloat16 [4096, 2048], P(('grp', 'seq')), may hold values from -6 to 6
Outputs:
- layer_out: bfloat16 [4096, 2048], P(('grp', 'seq'))
- tokens_grad: bfloat16 [4096, 2048], P(('grp', 'seq'))
- gains_grad: float32 [2, 2048], replicated
- biases_grad: float32 [2, 2048], replicated
- mix_grad: float32 [2048, 3, 2048], P(None, None, 'seq')
- mix_bias_grad: float32 [3, 2048], P(None, 'seq')
- out_grad: float32 [2048, 2048], P('seq')
- gate_up_grad: float32 [2048, 2, 5632], P(None, None, 'seq')
- down_grad: float32 [5632, 2048], P('seq')
Inputs may be any that keep to these rules, and one draw needn't show every extreme that they name: `row_lengths`: rows 0 to 1 are 1024 long; every other row's length is a multiple of 128 and at most 256. `row_group`: each of rows 0 to 1 fills a group alone; every other group holds exactly three of the other rows.
All inputs are finite; a program needn't handle non-finite values.
Results may differ from a plain program's by a relative error of at most 0.02.
Values may be sent and summed in bfloat16 or wider, within the bound.
A program may use at most 320 MiB of HBM per device.

v0:
```python
import math
import jax
import jax.numpy as jnp
from jax import lax
from jax.sharding import PartitionSpec as P

HEAD_DIM = 64
ROT = 16
EPS = 1e-05
NEG = -1e30
BASE = 10000.0


def layer_norm(values, gain, bias):
    centered = values - jnp.mean(values, axis=-1, keepdims=True)
    scale = lax.rsqrt(jnp.mean(centered * centered, axis=-1, keepdims=True) + EPS)
    unit = centered * scale
    return (unit * gain + bias, unit, scale)


def norm_back(incoming, unit, scale, gain):
    along = incoming * gain
    inner = jnp.mean(along, axis=-1, keepdims=True)
    cross = jnp.mean(along * unit, axis=-1, keepdims=True)
    return (
        scale * (along - inner - unit * cross),
        jnp.sum(incoming * unit, axis=0),
        jnp.sum(incoming, axis=0),
    )


def rotate(values, where, sign):
    half = ROT // 2
    freq = BASE ** (-jnp.arange(half, dtype=jnp.float32) / half)
    angle = where.astype(jnp.float32)[:, None] * freq[None, :]
    cosine = jnp.cos(angle)[:, None, :]
    sine = sign * jnp.sin(angle)[:, None, :]
    first = values[..., :half]
    second = values[..., half:ROT]
    return jnp.concatenate(
        [first * cosine - second * sine, second * cosine + first * sine, values[..., ROT:]], axis=-1
    )


def unrotate(lowered, where):
    wide = lowered.astype(jnp.float32)
    turned = jnp.stack(
        [rotate(wide[:, 0], where, -1.0), rotate(wide[:, 1], where, -1.0), wide[:, 2]], axis=1
    )
    return turned.reshape(lowered.shape[0], 3, -1).astype(jnp.bfloat16)


def slot_rows(row_lengths, row_group, group, slots):
    order = jnp.arange(row_lengths.shape[0], dtype=jnp.int32)
    same = row_group == group
    earlier = (order[:, None] > order[None, :]) & same[None, :]
    begin = jnp.sum(jnp.where(earlier, row_lengths[None, :], 0), axis=1)
    finish = begin + row_lengths
    inside = same[None, :] & (slots[:, None] >= begin[None, :]) & (slots[:, None] < finish[None, :])
    label = jnp.sum(jnp.where(inside, order[None, :] + 1, 0), axis=1) - 1
    offset = jnp.sum(jnp.where(inside, slots[:, None] - begin[None, :], 0), axis=1)
    load = jnp.sum(jnp.where(same, row_lengths, 0))
    return (label, jnp.where(label < 0, slots - load, offset))


def block_scores(query, key, label, start, block):
    part = lax.dynamic_slice_in_dim(query, start, block, 0)
    rows = start + jnp.arange(block, dtype=jnp.int32)
    columns = jnp.arange(label.shape[0], dtype=jnp.int32)
    label_rows = lax.dynamic_slice_in_dim(label, start, block, 0)
    allowed = (label_rows[:, None] == label[None, :]) & (rows[:, None] >= columns[None, :])
    scores = jnp.einsum("qhe,khe->hqk", part, key, preferred_element_type=jnp.float32) * (
        1.0 / math.sqrt(query.shape[-1])
    )
    return (part, jnp.where(allowed[None], scores, NEG))


def attend(query, key, value, label, block):

    def one_block(index):
        part, scores = block_scores(query, key, label, index * block, block)
        top = jnp.max(scores, axis=-1, keepdims=True)
        weights = jnp.exp(scores - top)
        totals = jnp.sum(weights, axis=-1, keepdims=True)
        probs = (weights / totals).astype(jnp.bfloat16)
        mixed = jnp.einsum("hqk,khe->qhe", probs, value, preferred_element_type=jnp.float32)
        return (mixed, top[..., 0] + jnp.log(totals[..., 0]))

    mixed, log_totals = lax.map(one_block, jnp.arange(query.shape[0] // block, dtype=jnp.int32))
    return (mixed.reshape(query.shape), log_totals)


def attend_back(query, key, value, label, log_totals, mixed_back, block):
    scale = 1.0 / math.sqrt(query.shape[-1])

    def one_block(carry, index):
        key_back, value_back = carry
        start = index * block
        part, scores = block_scores(query, key, label, start, block)
        back_part = lax.dynamic_slice_in_dim(mixed_back, start, block, 0)
        probs = jnp.exp(scores - log_totals[index][..., None])
        value_back = value_back + jnp.einsum(
            "hqk,qhe->khe",
            probs.astype(jnp.bfloat16),
            back_part,
            preferred_element_type=jnp.float32,
        )
        probs_back = jnp.einsum(
            "qhe,khe->hqk", back_part, value, preferred_element_type=jnp.float32
        )
        inner = jnp.sum(probs_back * probs, axis=-1, keepdims=True)
        score_back = (probs * (probs_back - inner)).astype(jnp.bfloat16)
        query_back = (
            jnp.einsum("hqk,khe->qhe", score_back, key, preferred_element_type=jnp.float32) * scale
        )
        key_back = (
            key_back
            + jnp.einsum("hqk,qhe->khe", score_back, part, preferred_element_type=jnp.float32)
            * scale
        )
        return ((key_back, value_back), query_back)

    empty = jnp.zeros(key.shape, jnp.float32)
    (key_back, value_back), query_back = lax.scan(
        one_block, (empty, empty), jnp.arange(query.shape[0] // block, dtype=jnp.int32)
    )
    return (query_back.reshape(query.shape), key_back, value_back)


def silu_parts(gate_up):
    gate = gate_up[:, 0]
    upper = gate_up[:, 1]
    sigma = jax.nn.sigmoid(gate)
    return (gate * sigma * upper, gate, upper, sigma)


def gate_back(hidden_back, gate, upper, sigma):
    gate_part = hidden_back * upper * sigma * (1.0 + gate * (1.0 - sigma))
    up_part = hidden_back * gate * sigma
    return jnp.stack([gate_part, up_part], axis=1).astype(jnp.bfloat16)


def gather_rows(values):
    return lax.all_gather(values, "seq", axis=0, tiled=True)


def summed_rows(product, left):
    return lax.psum_scatter(
        product(left).astype(jnp.bfloat16), "seq", scatter_dimension=0, tiled=True
    ).astype(jnp.float32)


def on_device(
    tokens,
    norm_gains,
    norm_biases,
    mix_weight,
    mix_bias,
    out_weight,
    gate_up_weight,
    down_weight,
    row_lengths,
    row_group,
    cotangent,
):
    seq_count = lax.axis_size("seq")
    shard = lax.axis_index("seq")
    group = lax.axis_index("grp")
    slots_dev = tokens.shape[0]
    width = tokens.shape[1]
    group_slots = slots_dev * seq_count
    block = min(512, group_slots)
    local_width = width // seq_count
    local_heads = local_width // HEAD_DIM
    mine = shard * slots_dev + jnp.arange(slots_dev, dtype=jnp.int32)
    label_mine, place_mine = slot_rows(row_lengths, row_group, group, mine)
    label_all, place_all = slot_rows(
        row_lengths, row_group, group, jnp.arange(group_slots, dtype=jnp.int32)
    )
    inputs = tokens.astype(jnp.float32)
    upstream = cotangent.astype(jnp.float32) * (label_mine >= 0).astype(jnp.float32)[:, None]
    upstream_low = upstream.astype(jnp.bfloat16)
    normed, unit_one, scale_one = layer_norm(inputs, norm_gains[0], norm_biases[0])
    normed_low = normed.astype(jnp.bfloat16)
    mix_full, bias_full, out_full = (
        lax.all_gather(mix_weight, "seq", axis=2, tiled=True),
        lax.all_gather(mix_bias, "seq", axis=1, tiled=True),
        lax.all_gather(out_weight, "seq", axis=0, tiled=True),
    )
    mixin = jnp.einsum(
        "td,dcf->tcf", normed_low, mix_full, preferred_element_type=jnp.float32
    ) + bias_full.astype(jnp.float32)
    heads_in = mixin.reshape(slots_dev, 3, width // HEAD_DIM, HEAD_DIM)
    sending = jnp.stack(
        [
            rotate(heads_in[:, 0], place_mine, 1.0),
            rotate(heads_in[:, 1], place_mine, 1.0),
            heads_in[:, 2],
        ],
        axis=1,
    ).astype(jnp.bfloat16)
    arrived = lax.all_to_all(
        sending.reshape(slots_dev, 3, seq_count, local_width),
        "seq",
        split_axis=2,
        concat_axis=0,
        tiled=True,
    )
    arrived = arrived.reshape(group_slots, 3, local_heads, HEAD_DIM)
    query, key, value = (arrived[:, 0], arrived[:, 1], arrived[:, 2])
    mixed, log_totals = attend(query, key, value, label_all, block)
    attended = lax.all_to_all(
        mixed.reshape(group_slots, local_width).astype(jnp.bfloat16),
        "seq",
        split_axis=0,
        concat_axis=1,
        tiled=True,
    )
    resid = inputs + jnp.dot(attended, out_full, preferred_element_type=jnp.float32)
    normed_two, unit_two, scale_two = layer_norm(resid, norm_gains[1], norm_biases[1])
    normed_two_all = gather_rows(normed_two.astype(jnp.bfloat16))
    gate_up = jnp.einsum(
        "td,dcf->tcf", normed_two_all, gate_up_weight, preferred_element_type=jnp.float32
    )
    hidden, gate, upper, sigma = silu_parts(gate_up)
    hidden_low = hidden.astype(jnp.bfloat16)

    def down_product(part):
        return jnp.dot(part, down_weight, preferred_element_type=jnp.float32)

    layer_out = resid + summed_rows(down_product, hidden_low)
    upstream_all = gather_rows(upstream_low)
    down_shard = jnp.einsum(
        "tf,td->fd", hidden_low, upstream_all, preferred_element_type=jnp.float32
    )
    hidden_back = jnp.einsum(
        "td,fd->tf", upstream_all, down_weight, preferred_element_type=jnp.float32
    )
    gate_up_back = gate_back(hidden_back, gate, upper, sigma)
    gate_up_shard = jnp.einsum(
        "td,tcf->dcf", normed_two_all, gate_up_back, preferred_element_type=jnp.float32
    )

    def gate_up_product(part):
        return jnp.einsum("tcf,dcf->td", part, gate_up_weight, preferred_element_type=jnp.float32)

    normed_two_back = summed_rows(gate_up_product, gate_up_back)
    resid_part, gain_two, bias_two = norm_back(normed_two_back, unit_two, scale_two, norm_gains[1])
    resid_back = upstream + resid_part
    branch_low = resid_back.astype(jnp.bfloat16)
    out_term = jnp.einsum("te,td->ed", attended, branch_low, preferred_element_type=jnp.float32)
    attended_back = jnp.einsum(
        "td,ed->te", branch_low, out_full, preferred_element_type=jnp.float32
    ).astype(jnp.bfloat16)
    heads_back = lax.all_to_all(
        attended_back, "seq", split_axis=1, concat_axis=0, tiled=True
    ).reshape(group_slots, local_heads, HEAD_DIM)
    query_back, key_back, value_back = attend_back(
        query, key, value, label_all, log_totals, heads_back, block
    )
    lowered = (
        jnp.stack([query_back, key_back, value_back], axis=1)
        .astype(jnp.bfloat16)
        .reshape(group_slots, 3, 1, local_width)
    )
    returned = lax.all_to_all(lowered, "seq", split_axis=0, concat_axis=2, tiled=True).reshape(
        slots_dev, 3, width // HEAD_DIM, HEAD_DIM
    )
    mixin_back = unrotate(returned, place_mine)
    mix_term = jnp.einsum("td,tcf->dcf", normed_low, mixin_back, preferred_element_type=jnp.float32)
    bias_term = jnp.sum(mixin_back, axis=0, dtype=jnp.float32)
    normed_back = jnp.einsum(
        "tcf,dcf->td", mixin_back, mix_full, preferred_element_type=jnp.float32
    )
    mix_shard, bias_shard, out_shard = (
        lax.psum_scatter(
            mix_term.astype(jnp.bfloat16), "seq", scatter_dimension=2, tiled=True
        ).astype(jnp.float32),
        lax.psum_scatter(
            bias_term.astype(jnp.bfloat16), "seq", scatter_dimension=1, tiled=True
        ).astype(jnp.float32),
        lax.psum_scatter(
            out_term.astype(jnp.bfloat16), "seq", scatter_dimension=0, tiled=True
        ).astype(jnp.float32),
    )
    tokens_part, gain_one, bias_one = norm_back(normed_back, unit_one, scale_one, norm_gains[0])
    tokens_grad = (resid_back + tokens_part).astype(jnp.bfloat16)
    mix_grad, mix_bias_grad, out_grad, gate_up_grad, down_grad = (
        lax.psum(mix_shard.astype(jnp.bfloat16), "grp").astype(jnp.float32),
        lax.psum(bias_shard.astype(jnp.bfloat16), "grp").astype(jnp.float32),
        lax.psum(out_shard.astype(jnp.bfloat16), "grp").astype(jnp.float32),
        lax.psum(gate_up_shard.astype(jnp.bfloat16), "grp").astype(jnp.float32),
        lax.psum(down_shard.astype(jnp.bfloat16), "grp").astype(jnp.float32),
    )
    gains_grad, biases_grad = lax.psum(
        (jnp.stack([gain_one, gain_two]), jnp.stack([bias_one, bias_two])), ("grp", "seq")
    )
    return (
        layer_out.astype(jnp.bfloat16),
        tokens_grad,
        gains_grad,
        biases_grad,
        mix_grad,
        mix_bias_grad,
        out_grad,
        gate_up_grad,
        down_grad,
    )


def solution(mesh):
    placed = (
        P(("grp", "seq"), None),
        P(),
        P(),
        P(None, None, "seq"),
        P(None, "seq"),
        P("seq", None),
        P(None, None, "seq"),
        P("seq", None),
        P(),
        P(),
        P(("grp", "seq"), None),
    )
    return jax.shard_map(
        on_device,
        mesh=mesh,
        in_specs=placed,
        out_specs=(
            P(("grp", "seq"), None),
            P(("grp", "seq"), None),
            P(),
            P(),
            P(None, None, "seq"),
            P(None, "seq"),
            P("seq", None),
            P(None, None, "seq"),
            P("seq", None),
        ),
        check_vma=False,
    )
```

profile of v0, /device:TPU:0, one launch (start us, length us, event | category | flops | bytes accessed | tf_op | source)
XLA Modules:
  0.0 1248.3 jit_solution(738130817734868844)
XLA Ops:
  9.5 10.4 all_gather.16
  21.9 121.0 %all-gather.5.cloned.1.call-done = bf16[2048,3,2048]{2,0,1:T(8,128)(2,1)} async-done(((bf16[2048,3,256]{2,0,1:T(8,128)(2,1)}), bf16[2048,3,2048]{2,0,1:T(8,128)(2,1)}) %all-gather.5.cloned.1.call-update) | async-done | bytes 25165840 | tf_op jit(solution)/shard_map/all_gather | solution.py:186
  143.0 13.4 %convolution_add_fusion = f32[128,3,2048]{2,0,1:T(8,128)} fusion(bf16[2048,3,2048]{2,0,1:T(8,128)(2,1)} %all-gather.5.cloned.1.call-done, f32[3,2048]{1,0:T(4,128)S(1)} %convert_element_type.139, bf16[128,2048]{1,0:T(8,128)(2,1)S(1)} %copy-done.5, f32[2048]{0:T(1024)S(1)} %bitcast.195, f32[2048]{0:T(1024)S(1)} %bitcast.191, f32[128]{0:T(128)S(1)} %add_rsqrt_fusion.1, ...), kind=kOutput, calls=%fused_computation.63 | convolution fusion | flops 3223584768 | bytes 28877824 | tf_op jit(solution)/shard_map/td,dcf->tcf/dot_general | solution.py:190
  169.3 35.6 %all-to-all-done = bf16[128,3,8,256]{0,3,1,2:T(8,128)(2,1)} async-done(((bf16[128,3,8,256]{0,3,1,2:T(8,128)(2,1)}), bf16[128,3,8,256]{0,3,1,2:T(8,128)(2,1)}, u32[]{:S(2)}, u32[]{:S(2)}) %all-to-all-start) | async-done | bytes 1572896 | tf_op jit(solution)/shard_map/all_to_all | solution.py:202
  215.6 21.5 %while.27 = (s32[]{:T(128)}, bf16[2,512,4,64]{1,3,2,0:T(8,128)(2,1)}, f32[2,4,512]{2,1,0:T(4,128)S(1)}, s32[2]{0:T(128)S(1)}, s32[1024]{0:T(1024)S(1)}, /*index=...) while((s32[]{:T(128)}, ...), condition=%wide.region_10.11_spmd, body=%wide.region_7.10_spmd.sunk | while | flops 563608064 | bytes 35469596 | solution.py:89
  247.8 9.7 all-to-all-done.1
  266.9 33.4 %all-gather.9.cloned.1.call-done = bf16[1024,2048]{1,0:T(8,128)(2,1)} async-done(((bf16[128,2048]{1,0:T(8,128)(2,1)}), bf16[1024,2048]{1,0:T(8,128)(2,1)}) %all-gather.9.cloned.1.call-update) | async-done | bytes 4194320 | tf_op jit(solution)/shard_map/all_gather | solution.py:144
  300.4 11.0 fusion.39
  311.4 28.1 %all-gather.11.cloned.1.call-done = bf16[1024,2048]{1,0:T(8,128)(2,1)} async-done(((bf16[128,2048]{1,0:T(8,128)(2,1)}), bf16[1024,2048]{1,0:T(8,128)(2,1)}) %all-gather.11.cloned.1.call-update) | async-done | bytes 4194320 | tf_op jit(solution)/shard_map/all_gather | solution.py:144
  339.5 8.3 fusion.45
  349.4 11.0 bitcast_convert_fusion
  366.9 45.0 %reduce-scatter.10.cloned.1.call-done = bf16[128,2048]{1,0:T(8,128)(2,1)} async-done(((bf16[1024,2048]{1,0:T(8,128)(2,1)}), bf16[128,2048]{1,0:T(8,128)(2,1)}) %reduce-scatter.10.cloned.1.call-update) | async-done | bytes 524304 | tf_op jit(solution)/shard_map/reduce_scatter | solution.py:148
  414.0 53.4 %reduce-scatter.8.cloned.1.call-done = bf16[128,2048]{1,0:T(8,128)(2,1)} async-done(((bf16[1024,2048]{1,0:T(8,128)(2,1)}), bf16[128,2048]{1,0:T(8,128)(2,1)}) %reduce-scatter.8.cloned.1.call-update) | async-done | bytes 524304 | tf_op jit(solution)/shard_map/reduce_scatter | solution.py:148
  487.7 9.4 all-to-all-done.2
  501.1 31.6 %while.28 = (s32[]{:T(128)}, f32[1024,4,64]{0,2,1:T(8,128)S(1)}, f32[1024,4,64]{0,2,1:T(8,128)}, bf16[2,512,4,64]{1,3,2,0:T(8,128)(2,1)}, s32[2]{0:T(128)S(1)}, ...) while((s32[]{:T(128)}, f32[1024,4,64]{0,2,1:T(8,128)S(1)}, ...), condition=%wide.region_19.20_spmd.clone, body=%wide.region_17.19_spmd.clone.sunk | while | flops 1376647680 | bytes 87103920 | solution.py:124
  540.5 29.5 %all_to_all.56 = bf16[1024,3,1,256]{3,1,2,0:T(4,128)(2,1)S(1)} all-to-all(bf16[1024,3,1,256]{3,1,2,0:T(4,128)(2,1)S(1)} %copy.98), channel_id=1, replica_groups=mesh['grp'=4,'seq'=8] {'seq'}, dimensions={0} | all-to-all | bytes 3145728 | tf_op jit(solution)/shard_map/all_to_all | solution.py:266
  578.5 12.0 convolution_convert_fusion
  590.6 10.8 convolution_convert_fusion.2
  603.1 8.9 convolution_convert_fusion.4
  612.0 134.7 %reduce-scatter.12.cloned.1.call-done = bf16[2048,3,256]{2,0,1:T(8,128)(2,1)} async-done(((bf16[2048,3,2048]{2,0,1:T(8,128)(2,1)}), bf16[2048,3,256]{2,0,1:T(8,128)(2,1)}) %reduce-scatter.12.cloned.1.call-update) | async-done | bytes 3145744 | tf_op jit(solution)/shard_map/reduce_scatter | solution.py:276
  746.7 14.6 %fusion.59 = (f32[2048]{0:T(1024)S(1)}, f32[128]{0:T(128)S(1)}, f32[128]{0:T(128)S(1)}, f32[2048]{0:T(1024)S(1)}, f32[128,2048]{1,0:T(8,128)}) fusion(bf16[128,2048]{1,0:T(8,128)(2,1)S(1)} %copy-done.6, f32[128]{0:T(128)S(1)} %copy-done.35, f32[128]{0:T(128)S(1)} %copy-done.33, f32[2048]{0:T(1024)S(1)} %bitcast.193, ...), kind=kOutput, calls=%fused_computation.93 | convolution fusion | flops 3225415680 | bytes 28338176 | tf_op jit(solution)/shard_map/tcf,dcf->td/dot_general | solution.py:272
  761.4 40.2 %all-reduce = (f32[2,2048]{1,0:T(2,128)}, f32[2,2048]{1,0:T(2,128)}) all-reduce(f32[2,2048]{1,0:T(2,128)S(1)} %pad_maximum_fusion.10, f32[2,2048]{1,0:T(2,128)S(1)} %pad_maximum_fusion.11), channel_id=1, replica_groups=mesh['grp'=4,'seq'=8] {'grp','seq'}, use_global_device_ids=true, to_apply=%region_24.25 | all-reduce | flops 8192 | bytes 65536 | tf_op jit(solution)/shard_map/psum | solution.py:295
  805.0 12.3 psum.52
  817.9 407.1 %all-reduce.4.cloned.1.call-done = (bf16[2048,3,256]{2,0,1:T(8,128)(2,1)}, bf16[256,2048]{1,0:T(8,128)(2,1)}, bf16[2048,2,704]{0,2,1:T(8,128)(2,1)}, bf16[704,2048]{1,0:T(8,128)(2,1)}) async-done(((bf16[2048,3,256]{2,0,1:T(8,128)(2,1)}, bf16[256,2048]{1,0:T(8,128)(2,1)}, bf16[2048,2,704]{0,2,1:T(8,128)(2,1)}, bf16[704,2048]{1,0:T(8,128)(2,1)}), (bf16[2048,3,256]{2,0,1:T(8,128)(2,1)}, ...) | async-done | bytes 12845072 | tf_op jit(solution)/shard_map/psum | solution.py:289
  (256 shorter events, 166.6 us)
Async XLA Ops:
  7.2 332.3 %copy-start = (bf16[704,2048]{1,0:T(8,128)(2,1)S(1)}, bf16[704,2048]{1,0:T(8,128)(2,1)}, u32[]{:S(2)}) copy-start(bf16[704,2048]{1,0:T(8,128)(2,1)} %param.22) | copy-start | bytes 8650756
  7.3 135.7 %all-gather.5.cloned.1.call-start = ((), (), s32[]{:S(2)}) async-start(), calls=%async_computation.9 | async-start | bytes 28311552 | tf_op jit(solution)/shard_map/all_gather | solution.py:186
  8.0 239.8 %all-gather.7.cloned.1.call-start = ((), (), s32[]{:S(2)}) async-start(), calls=%async_computation.10 | async-start | bytes 9437184 | tf_op jit(solution)/shard_map/all_gather | solution.py:188
  20.2 136.2 %copy-start.32 = (f32[128]{0:T(128)}, f32[128]{0:T(128)S(1)}, u32[]{:S(2)}) copy-start(f32[128]{0:T(128)S(1)} %broadcast_multiply_fusion.6) | copy-start | bytes 1540
  20.5 135.9 %copy-start.34 = (f32[128]{0:T(128)}, f32[128]{0:T(128)S(1)}, u32[]{:S(2)}) copy-start(f32[128]{0:T(128)S(1)} %add_rsqrt_fusion.1) | copy-start | bytes 1540
  21.9 141.2 %copy-start.25 = (f32[128,8]{0,1:T(8,128)}, f32[128,8]{0,1:T(8,128)S(1)}, u32[]{:S(2)}) copy-start(f32[128,8]{0,1:T(8,128)S(1)} %get-tuple-element.253) | copy-start | bytes 12292
  21.9 134.5 %copy-start.21 = (f32[1,2048]{1,0:T(1,128)}, f32[1,2048]{1,0:T(1,128)S(1)}, u32[]{:S(2)}) copy-start(f32[1,2048]{1,0:T(1,128)S(1)} %get-tuple-element.244) | copy-start | bytes 24580
  21.9 134.4 %copy-start.23 = (f32[1,2048]{1,0:T(1,128)}, f32[1,2048]{1,0:T(1,128)S(1)}, u32[]{:S(2)}) copy-start(f32[1,2048]{1,0:T(1,128)S(1)} %get-tuple-element.246) | copy-start | bytes 24580
  164.7 40.2 %all-to-all-start = ((bf16[128,3,8,256]{0,3,1,2:T(8,128)(2,1)}), bf16[128,3,8,256]{0,3,1,2:T(8,128)(2,1)}, u32[]{:S(2)}, u32[]{:S(2)}) async-start(bf16[128,3,8,256]{0,3,1,2:T(8,128)(2,1)} %copy.91), calls=%async_computation | async-start | bytes 3145728 | tf_op jit(solution)/shard_map/all_to_all | solution.py:202
  243.5 13.9 %all-to-all-start.1 = ((bf16[8,128,256]{1,2,0:T(8,128)(2,1)}), bf16[8,128,256]{1,2,0:T(8,128)(2,1)}, u32[]{:S(2)}, u32[]{:S(2)}) async-start(bf16[8,128,256]{1,2,0:T(8,128)(2,1)} %copy.94), calls=%async_computation.1 | async-start | bytes 1048576 | tf_op jit(solution)/shard_map/all_to_all | solution.py:212
  247.7 52.7 %all-gather.9.cloned.1.call-start = ((), (), s32[]{:S(2)}) async-start(), calls=%async_computation.11 | async-start | bytes 4718592 | tf_op jit(solution)/shard_map/all_gather | solution.py:144
  264.4 75.0 %all-gather.11.cloned.1.call-start = ((), (), s32[]{:S(2)}) async-start(), calls=%async_computation.13 | async-start | bytes 4718592 | tf_op jit(solution)/shard_map/all_gather | solution.py:144
  266.5 145.4 %reduce-scatter.10.cloned.1.call-start = ((), (), s32[]{:S(2)}) async-start(), calls=%async_computation.14 | async-start | bytes 4718592 | tf_op jit(solution)/shard_map/reduce_scatter | solution.py:148
  360.4 107.0 %reduce-scatter.8.cloned.1.call-start = ((), (), s32[]{:S(2)}) async-start(), calls=%async_computation.12 | async-start | bytes 4718592 | tf_op jit(solution)/shard_map/reduce_scatter | solution.py:148
  366.8 45.0 %copy-start.4 = (f32[128,2048]{1,0:T(8,128)S(1)}, f32[128,2048]{1,0:T(8,128)}, u32[]{:S(2)}) copy-start(f32[128,2048]{1,0:T(8,128)} %copy-done.3) | copy-start | bytes 3145732
  366.8 100.5 %copy-start.18 = (bf16[128,2048]{1,0:T(8,128)(2,1)S(1)}, bf16[128,2048]{1,0:T(8,128)(2,1)}, u32[]{:S(2)}) copy-start(bf16[128,2048]{1,0:T(8,128)(2,1)} %param.25) | copy-start | bytes 1572868
  366.9 245.1 %reduce-scatter.14.cloned.1.call-start = ((), (), s32[]{:S(2)}) async-start(), calls=%async_computation.16 | async-start | bytes 9437184 | tf_op jit(solution)/shard_map/reduce_scatter | solution.py:282
  483.1 18.0 %copy-start.2 = (bf16[1024,4,64]{0,2,1:T(8,128)(2,1)S(1)}, bf16[1024,4,64]{0,2,1:T(8,128)(2,1)}, u32[]{:S(2)}) copy-start(bf16[1024,4,64]{0,2,1:T(8,128)(2,1)} %get-tuple-element.490) | copy-start | bytes 1572868
  483.1 18.0 %copy-start.8 = (bf16[1024,4,64]{0,2,1:T(8,128)(2,1)S(1)}, bf16[1024,4,64]{0,2,1:T(8,128)(2,1)}, u32[]{:S(2)}) copy-start(bf16[1024,4,64]{0,2,1:T(8,128)(2,1)} %get-tuple-element.491) | copy-start | bytes 1572868
  484.0 13.2 %all-to-all-start.2 = ((bf16[128,8,256]{2,0,1:T(8,128)(2,1)}), bf16[128,8,256]{2,0,1:T(8,128)(2,1)S(1)}, u32[]{:S(2)}, u32[]{:S(2)}) async-start(bf16[128,8,256]{2,0,1:T(8,128)(2,1)} %bitcast.142), calls=%async_computation.4 | async-start | bytes 1048576 | tf_op jit(solution)/shard_map/all_to_all | solution.py:255
  487.5 259.2 %reduce-scatter.12.cloned.1.call-start = ((), (), s32[]{:S(2)}) async-start(), calls=%async_computation.15 | async-start | bytes 28311552 | tf_op jit(solution)/shard_map/reduce_scatter | solution.py:276
  590.5 213.5 %reduce-scatter.16.cloned.1.call-start = ((), (), s32[]{:S(2)}) async-start(), calls=%async_computation.17 | async-start | bytes 589824
  602.8 622.3 %all-reduce.4.cloned.1.call-start = ((), (), s32[]{:S(2)}) async-start(), calls=%async_computation.18 | async-start | bytes 25690112 | tf_op jit(solution)/shard_map/psum | solution.py:289
  746.7 54.9 %copy-start.10 = (f32[128,2048]{1,0:T(8,128)S(1)}, f32[128,2048]{1,0:T(8,128)}, u32[]{:S(2)}) copy-start(f32[128,2048]{1,0:T(8,128)} %copy-done.9) | copy-start | bytes 3145732
  (40 other events, 156.5 us)
Sparse Core Ops, SparseCore 0:
  10.0 132.9 all-gather.4
  144.9 68.7 all-gather.6
  264.5 35.7 all-gather.8
  302.7 36.7 all-gather.10
  360.5 51.3 reduce-scatter.9
  416.0 51.2 reduce-scatter.7
  476.9 71.4 reduce-scatter.13
  590.6 155.9 reduce-scatter.11
  750.0 34.2 reduce-scatter.15
  788.2 436.8 all-reduce.3
where the time goes:
time: 1250 us
  waiting for transfers between devices  879 us (70%)
  matrix products  145 us (12%)
  blocking collectives  92.4 us (7%)
  local copies, waits for them, and re-layouts  49.7 us (4%)
  other arithmetic  47.1 us (4%)
  between operations  15.2 us (1%)
  starting transfers between devices  13.4 us (1%)
    psum x1, waiting for transfers between devices, on_device(): lax.psum(mix_shard.astype(jnp.bfloat16), 'grp').astype(jnp.float32)  407 us
    reduce_scatter x1, waiting for transfers between devices, on_device(): lax.psum_scatter(mix_term.astype(jnp.bfloat16), 'seq', scatter_dimension=...  135 us
    all_gather x1, waiting for transfers between devices, on_device(): lax.all_gather(mix_weight, 'seq', axis=2, tiled=True)  121 us
    reduce_scatter x2, waiting for transfers between devices, summed_rows(): lax.psum_scatter(product(left).astype(jnp.bfloat16), 'seq', scatter_dimen...  98.3 us
    all_gather x2, waiting for transfers between devices, gather_rows(): return lax.all_gather(values, 'seq', axis=0, tiled=True)  61.5 us
    psum x1, blocking collectives, on_device(): lax.psum((jnp.stack([gain_one, gain_two]), jnp.stack([bias_one, bias_two]...  40.2 us
    all_to_all x1, waiting for transfers between devices, on_device(): lax.all_to_all(sending.reshape(slots_dev, 3, seq_count, local_width), 'se...  35.6 us
    all_to_all x1, blocking collectives, on_device(): lax.all_to_all(lowered, 'seq', split_axis=0, concat_axis=2, tiled=True)  29.5 us
  transfers between devices with their start and end apart: 13, of which 10 were waited for; matrix products, arithmetic and copies ran while one was open for 15% of the time, Pallas kernels for 0%

commit v1 on v0

--- a/solution.py
+++ b/solution.py
@@ -286,7 +286,7 @@
     tokens_part, gain_one, bias_one = norm_back(normed_back, unit_one, scale_one, norm_gains[0])
     tokens_grad = (resid_back + tokens_part).astype(jnp.bfloat16)
     mix_grad, mix_bias_grad, out_grad, gate_up_grad, down_grad = (
-        lax.psum(mix_shard.astype(jnp.bfloat16), "grp").astype(jnp.float32),
+        jnp.sum(lax.all_gather(mix_shard.astype(jnp.bfloat16), "grp"), axis=0).astype(jnp.float32),
         lax.psum(bias_shard.astype(jnp.bfloat16), "grp").astype(jnp.float32),
         lax.psum(out_shard.astype(jnp.bfloat16), "grp").astype(jnp.float32),
         lax.psum(gate_up_shard.astype(jnp.bfloat16), "grp").astype(jnp.float32),

time: 1250 us -> 1370 us (1.096)
  waiting for transfers between devices: 879 us -> 984 us
    all_gather x0 -> x1, waiting for transfers between devices: none -> 205 us  [on_device(): lax.all_gather(mix_shard.astype(jnp.bfloat16), 'grp')]
    psum x1, waiting for transfers between devices: 407 us -> 306 us  [on_device(): lax.psum(out_shard.astype(jnp.bfloat16), 'grp').astype(jnp.float32)]
  transfers between devices with their start and end apart: 13 -> 14, of which waited for: 10 -> 11; matrix products, arithmetic and copies ran while one was open for 15% -> 15% of each run, Pallas kernels for 0% -> 0%
where the time goes in v1:
time: 1370 us; the launch traced here: 1360 us
  waiting for transfers between devices  984 us (72%)
  matrix products  145 us (11%)
  blocking collectives  91.7 us (7%)
  other arithmetic  58.7 us (4%)
  local copies, waits for them, and re-layouts  49.4 us (4%)
  between operations  14.9 us (1%)
    psum x1, waiting for transfers between devices, on_device(): lax.psum(out_shard.astype(jnp.bfloat16), 'grp').astype(jnp.float32)  306 us
    all_gather x1, waiting for transfers between devices, on_device(): lax.all_gather(mix_shard.astype(jnp.bfloat16), 'grp')  205 us
    reduce_scatter x1, waiting for transfers between devices, on_device(): lax.psum_scatter(mix_term.astype(jnp.bfloat16), 'seq', scatter_dimension=...  135 us
    all_gather x1, waiting for transfers between devices, on_device(): lax.all_gather(mix_weight, 'seq', axis=2, tiled=True)  121 us
    reduce_scatter x2, waiting for transfers between devices, summed_rows(): lax.psum_scatter(product(left).astype(jnp.bfloat16), 'seq', scatter_dimen...  98.3 us
    all_gather x2, waiting for transfers between devices, gather_rows(): return lax.all_gather(values, 'seq', axis=0, tiled=True)  61.5 us
    psum x1, blocking collectives, on_device(): lax.psum((jnp.stack([gain_one, gain_two]), jnp.stack([bias_one, bias_two]...  40.2 us
    all_to_all x1, waiting for transfers between devices, on_device(): lax.all_to_all(sending.reshape(slots_dev, 3, seq_count, local_width), 'se...  35.6 us
  transfers between devices with their start and end apart: 14, of which 11 were waited for; matrix products, arithmetic and copies ran while one was open for 15% of the time, Pallas kernels for 0%

profile of v1, /device:TPU:0, one launch (start us, length us, event | category | flops | bytes accessed | tf_op | source)
XLA Modules:
  0.0 1362.7 jit_solution(18211757739679225277)
XLA Ops:
  9.5 10.4 all_gather.22
  21.9 121.0 %all-gather.7.cloned.1.call-done = bf16[2048,3,2048]{2,0,1:T(8,128)(2,1)} async-done(((bf16[2048,3,256]{2,0,1:T(8,128)(2,1)}), bf16[2048,3,2048]{2,0,1:T(8,128)(2,1)}) %all-gather.7.cloned.1.call-update) | async-done | bytes 25165840 | tf_op jit(solution)/shard_map/all_gather | solution.py:186
  143.0 13.4 convolution_add_fusion
  169.3 35.6 %all-to-all-done = bf16[128,3,8,256]{0,3,1,2:T(8,128)(2,1)} async-done(((bf16[128,3,8,256]{0,3,1,2:T(8,128)(2,1)}), bf16[128,3,8,256]{0,3,1,2:T(8,128)(2,1)}, u32[]{:S(2)}, u32[]{:S(2)}) %all-to-all-start) | async-done | bytes 1572896 | tf_op jit(solution)/shard_map/all_to_all | solution.py:202
  215.6 21.5 %while.27 = (s32[]{:T(128)}, bf16[2,512,4,64]{1,3,2,0:T(8,128)(2,1)}, f32[2,4,512]{2,1,0:T(4,128)S(1)}, s32[2]{0:T(128)S(1)}, s32[1024]{0:T(1024)S(1)}, /*index=...) while((s32[]{:T(128)}, ...), condition=%wide.region_10.11_spmd, body=%wide.region_7.10_spmd.sunk | while | flops 563608064 | bytes 35469596 | solution.py:89
  247.8 9.7 all-to-all-done.1
  266.9 33.4 %all-gather.11.cloned.1.call-done = bf16[1024,2048]{1,0:T(8,128)(2,1)} async-done(((bf16[128,2048]{1,0:T(8,128)(2,1)}), bf16[1024,2048]{1,0:T(8,128)(2,1)}) %all-gather.11.cloned.1.call-update) | async-done | bytes 4194320 | tf_op jit(solution)/shard_map/all_gather | solution.py:144
  300.4 11.0 fusion.39
  311.4 28.1 %all-gather.13.cloned.1.call-done = bf16[1024,2048]{1,0:T(8,128)(2,1)} async-done(((bf16[128,2048]{1,0:T(8,128)(2,1)}), bf16[1024,2048]{1,0:T(8,128)(2,1)}) %all-gather.13.cloned.1.call-update) | async-done | bytes 4194320 | tf_op jit(solution)/shard_map/all_gather | solution.py:144
  349.4 11.0 bitcast_convert_fusion
  366.9 45.0 %reduce-scatter.10.cloned.1.call-done = bf16[128,2048]{1,0:T(8,128)(2,1)} async-done(((bf16[1024,2048]{1,0:T(8,128)(2,1)}), bf16[128,2048]{1,0:T(8,128)(2,1)}) %reduce-scatter.10.cloned.1.call-update) | async-done | bytes 524304 | tf_op jit(solution)/shard_map/reduce_scatter | solution.py:148
  414.0 53.4 %reduce-scatter.8.cloned.1.call-done = bf16[128,2048]{1,0:T(8,128)(2,1)} async-done(((bf16[1024,2048]{1,0:T(8,128)(2,1)}), bf16[128,2048]{1,0:T(8,128)(2,1)}) %reduce-scatter.8.cloned.1.call-update) | async-done | bytes 524304 | tf_op jit(solution)/shard_map/reduce_scatter | solution.py:148
  487.7 9.4 all-to-all-done.2
  501.1 31.0 %while.28 = (s32[]{:T(128)}, f32[1024,4,64]{0,2,1:T(8,128)S(1)}, f32[1024,4,64]{0,2,1:T(8,128)}, bf16[2,512,4,64]{1,3,2,0:T(8,128)(2,1)}, s32[2]{0:T(128)S(1)}, ...) while((s32[]{:T(128)}, f32[1024,4,64]{0,2,1:T(8,128)S(1)}, ...), condition=%wide.region_19.20_spmd.clone, body=%wide.region_17.19_spmd.clone.sunk | while | flops 1376647680 | bytes 87103920 | solution.py:124
  539.7 30.3 %all_to_all.56 = bf16[1024,3,1,256]{3,1,2,0:T(4,128)(2,1)S(1)} all-to-all(bf16[1024,3,1,256]{3,1,2,0:T(4,128)(2,1)S(1)} %copy.98), channel_id=1, replica_groups=mesh['grp'=4,'seq'=8] {'seq'}, dimensions={0} | all-to-all | bytes 3145728 | tf_op jit(solution)/shard_map/all_to_all | solution.py:266
  578.4 11.9 convolution_convert_fusion
  590.4 10.8 convolution_convert_fusion.2
  611.8 134.6 %reduce-scatter.12.cloned.1.call-done = bf16[2048,3,256]{2,0,1:T(8,128)(2,1)} async-done(((bf16[2048,3,2048]{2,0,1:T(8,128)(2,1)}), bf16[2048,3,256]{2,0,1:T(8,128)(2,1)}) %reduce-scatter.12.cloned.1.call-update) | async-done | bytes 3145744 | tf_op jit(solution)/shard_map/reduce_scatter | solution.py:276
  746.5 14.6 %fusion.59 = (f32[2048]{0:T(1024)S(1)}, f32[128]{0:T(128)S(1)}, f32[128]{0:T(128)S(1)}, f32[2048]{0:T(1024)S(1)}, f32[128,2048]{1,0:T(8,128)}) fusion(bf16[128,2048]{1,0:T(8,128)(2,1)S(1)} %copy-done.6, f32[128]{0:T(128)S(1)} %copy-done.34, f32[128]{0:T(128)S(1)} %copy-done.32, f32[2048]{0:T(1024)S(1)} %bitcast.195, ...), kind=kOutput, calls=%fused_computation.93 | convolution fusion | flops 3225415680 | bytes 28338176 | tf_op jit(solution)/shard_map/tcf,dcf->td/dot_general | solution.py:272
  761.2 40.2 %all-reduce = (f32[2,2048]{1,0:T(2,128)}, f32[2,2048]{1,0:T(2,128)}) all-reduce(f32[2,2048]{1,0:T(2,128)S(1)} %pad_maximum_fusion.10, f32[2,2048]{1,0:T(2,128)S(1)} %pad_maximum_fusion.11), channel_id=1, replica_groups=mesh['grp'=4,'seq'=8] {'grp','seq'}, use_global_device_ids=true, to_apply=%region_24.25 | all-reduce | flops 8192 | bytes 65536 | tf_op jit(solution)/shard_map/psum | solution.py:295
  804.8 10.9 psum.44
  816.3 306.4 %all-reduce.4.cloned.1.call-done = (bf16[256,2048]{1,0:T(8,128)(2,1)}, bf16[2048,2,704]{0,2,1:T(8,128)(2,1)}, bf16[704,2048]{1,0:T(8,128)(2,1)}) async-done(((bf16[256,2048]{1,0:T(8,128)(2,1)}, bf16[2048,2,704]{0,2,1:T(8,128)(2,1)}, bf16[704,2048]{1,0:T(8,128)(2,1)}), (bf16[256,2048]{1,0:T(8,128)(2,1)}, bf16[2048,2,704]{0,2,1:T(8,128)(2,1)}, bf16[704,2048]{1,0:T(8,128)(2,1)})) %all-reduce.4.cloned.1.call-update) | async-done | bytes 9699344 | tf_op jit(solution)/shard_map/psum | solution.py:291
  1136.0 205.5 %all-gather.15.cloned.1.call-done = bf16[8192,3,256]{2,0,1:T(8,128)(2,1)} async-done(((bf16[2048,3,256]{2,0,1:T(8,128)(2,1)}), bf16[8192,3,256]{2,0,1:T(8,128)(2,1)}) %all-gather.15.cloned.1.call-update) | async-done | bytes 12582928 | tf_op jit(solution)/shard_map/all_gather | solution.py:289
  1341.4 9.1 reduce_sum.216
  (258 shorter events, 185.9 us)
Async XLA Ops:
  7.2 332.3 %copy-start = (bf16[704,2048]{1,0:T(8,128)(2,1)S(1)}, bf16[704,2048]{1,0:T(8,128)(2,1)}, u32[]{:S(2)}) copy-start(bf16[704,2048]{1,0:T(8,128)(2,1)} %param.22) | copy-start | bytes 8650756
  7.3 135.7 %all-gather.7.cloned.1.call-start = ((), (), s32[]{:S(2)}) async-start(), calls=%async_computation.9 | async-start | bytes 28311552 | tf_op jit(solution)/shard_map/all_gather | solution.py:186
  8.0 239.8 %all-gather.9.cloned.1.call-start = ((), (), s32[]{:S(2)}) async-start(), calls=%async_computation.10 | async-start | bytes 9437184 | tf_op jit(solution)/shard_map/all_gather | solution.py:188
  20.2 136.2 %copy-start.31 = (f32[128]{0:T(128)}, f32[128]{0:T(128)S(1)}, u32[]{:S(2)}) copy-start(f32[128]{0:T(128)S(1)} %broadcast_multiply_fusion.6) | copy-start | bytes 1540
  20.5 135.9 %copy-start.33 = (f32[128]{0:T(128)}, f32[128]{0:T(128)S(1)}, u32[]{:S(2)}) copy-start(f32[128]{0:T(128)S(1)} %add_rsqrt_fusion.1) | copy-start | bytes 1540
  21.9 141.2 %copy-start.24 = (f32[128,8]{0,1:T(8,128)}, f32[128,8]{0,1:T(8,128)S(1)}, u32[]{:S(2)}) copy-start(f32[128,8]{0,1:T(8,128)S(1)} %get-tuple-element.252) | copy-start | bytes 12292
  21.9 134.5 %copy-start.20 = (f32[1,2048]{1,0:T(1,128)}, f32[1,2048]{1,0:T(1,128)S(1)}, u32[]{:S(2)}) copy-start(f32[1,2048]{1,0:T(1,128)S(1)} %get-tuple-element.243) | copy-start | bytes 24580
  21.9 134.4 %copy-start.22 = (f32[1,2048]{1,0:T(1,128)}, f32[1,2048]{1,0:T(1,128)S(1)}, u32[]{:S(2)}) copy-start(f32[1,2048]{1,0:T(1,128)S(1)} %get-tuple-element.245) | copy-start | bytes 24580
  164.7 40.2 %all-to-all-start = ((bf16[128,3,8,256]{0,3,1,2:T(8,128)(2,1)}), bf16[128,3,8,256]{0,3,1,2:T(8,128)(2,1)}, u32[]{:S(2)}, u32[]{:S(2)}) async-start(bf16[128,3,8,256]{0,3,1,2:T(8,128)(2,1)} %copy.91), calls=%async_computation | async-start | bytes 3145728 | tf_op jit(solution)/shard_map/all_to_all | solution.py:202
  243.5 13.9 %all-to-all-start.1 = ((bf16[8,128,256]{1,2,0:T(8,128)(2,1)}), bf16[8,128,256]{1,2,0:T(8,128)(2,1)}, u32[]{:S(2)}, u32[]{:S(2)}) async-start(bf16[8,128,256]{1,2,0:T(8,128)(2,1)} %copy.94), calls=%async_computation.1 | async-start | bytes 1048576 | tf_op jit(solution)/shard_map/all_to_all | solution.py:212
  247.7 52.7 %all-gather.11.cloned.1.call-start = ((), (), s32[]{:S(2)}) async-start(), calls=%async_computation.11 | async-start | bytes 4718592 | tf_op jit(solution)/shard_map/all_gather | solution.py:144
  264.4 75.0 %all-gather.13.cloned.1.call-start = ((), (), s32[]{:S(2)}) async-start(), calls=%async_computation.13 | async-start | bytes 4718592 | tf_op jit(solution)/shard_map/all_gather | solution.py:144
  266.5 145.4 %reduce-scatter.10.cloned.1.call-start = ((), (), s32[]{:S(2)}) async-start(), calls=%async_computation.14 | async-start | bytes 4718592 | tf_op jit(solution)/shard_map/reduce_scatter | solution.py:148
  360.4 107.0 %reduce-scatter.8.cloned.1.call-start = ((), (), s32[]{:S(2)}) async-start(), calls=%async_computation.12 | async-start | bytes 4718592 | tf_op jit(solution)/shard_map/reduce_scatter | solution.py:148
  366.8 45.0 %copy-start.4 = (f32[128,2048]{1,0:T(8,128)S(1)}, f32[128,2048]{1,0:T(8,128)}, u32[]{:S(2)}) copy-start(f32[128,2048]{1,0:T(8,128)} %copy-done.3) | copy-start | bytes 3145732
  366.8 100.5 %copy-start.17 = (bf16[128,2048]{1,0:T(8,128)(2,1)S(1)}, bf16[128,2048]{1,0:T(8,128)(2,1)}, u32[]{:S(2)}) copy-start(bf16[128,2048]{1,0:T(8,128)(2,1)} %param.25) | copy-start | bytes 1572868
  366.8 244.7 %reduce-scatter.14.cloned.1.call-start = ((), (), s32[]{:S(2)}) async-start(), calls=%async_computation.16 | async-start | bytes 9437184 | tf_op jit(solution)/shard_map/reduce_scatter | solution.py:282
  483.1 18.0 %copy-start.2 = (bf16[1024,4,64]{0,2,1:T(8,128)(2,1)S(1)}, bf16[1024,4,64]{0,2,1:T(8,128)(2,1)}, u32[]{:S(2)}) copy-start(bf16[1024,4,64]{0,2,1:T(8,128)(2,1)} %get-tuple-element.488) | copy-start | bytes 1572868
  483.9 13.2 all-to-all-start.2
  487.4 259.0 %reduce-scatter.12.cloned.1.call-start = ((), (), s32[]{:S(2)}) async-start(), calls=%async_computation.15 | async-start | bytes 28311552 | tf_op jit(solution)/shard_map/reduce_scatter | solution.py:276
  590.3 213.5 %reduce-scatter.16.cloned.1.call-start = ((), (), s32[]{:S(2)}) async-start(), calls=%async_computation.18 | async-start | bytes 589824
  602.6 520.1 %all-reduce.4.cloned.1.call-start = ((), (), s32[]{:S(2)}) async-start(), calls=%async_computation.19 | async-start | bytes 19398656 | tf_op jit(solution)/shard_map/psum | solution.py:291
  611.5 729.9 %all-gather.15.cloned.1.call-start = ((), (), s32[]{:S(2)}) async-start(), calls=%async_computation.17 | async-start | bytes 15728640 | tf_op jit(solution)/shard_map/all_gather | solution.py:289
  746.5 54.9 %copy-start.10 = (f32[128,2048]{1,0:T(8,128)S(1)}, f32[128,2048]{1,0:T(8,128)}, u32[]{:S(2)}) copy-start(f32[128,2048]{1,0:T(8,128)} %copy-done.9) | copy-start | bytes 3145732
  (40 other events, 171.5 us)
Sparse Core Ops, SparseCore 0:
  10.0 132.9 all-gather.6
  144.9 68.7 all-gather.8
  264.5 35.7 all-gather.10
  302.7 36.7 all-gather.12
  360.5 51.3 reduce-scatter.9
  416.0 51.2 reduce-scatter.7
  476.9 72.3 reduce-scatter.13
  590.5 155.9 reduce-scatter.11
  749.8 34.2 reduce-scatter.15
  788.0 334.6 all-reduce.3
  1124.3 217.1 all-gather.14
